TPU v7x, 256 devices: a whole 4x4x8 slice. The times are simulated.
256 devices in a mesh: tile: 64 (over x, z, core), rep: 4 (over y).
Axes of the slice: x: 4, y: 4, z: 8, core: 2. Of those that a mesh axis runs over, the one named last changes fastest.
Arguments:
- sequence_codes: int32 [41472], replicated, may hold values from 0 to 3
- pair_allowed: int32 [32768, 512], P('tile', 'rep'), may hold values 0 or 1
- stack_weight: float32 [4, 4], replicated, may hold values from 0.3 to 3
- hairpin_weight: float32 [4, 4], replicated, may hold values from 0.5 to 5
- loop_weight: float32 [31, 31], replicated, may hold values from 0.0005 to 0.01
- inner_pairs: float32 [32768, 542], P('tile'), may hold values from 0.1 to 10
- multi_left: float32 [32768, 16, 512], P('tile', None, 'rep'), may hold values from 0.1 to 10
- branch_right: float32 [64, 16, 512, 512], P('tile', None, 'rep'), may hold values from 1.2207031e-05 to 0.0012207031
Outputs:
- paired_window: float32 [32768, 512], P('tile', 'rep')
- multi_split: float32 [32768, 512], P('tile', 'rep')
All inputs are finite; a program needn't handle non-finite values. No bound on the sum of `pair_allowed` on one device may be relied on, other than what follows from the above.
Results may differ from a plain program's by a relative error of at most 0.0003.
Values sent between devices are 32-bit elements; how exact they have to be, the bound alone decides.
A program may use at most 192 MiB of HBM per device.

v0:
```python
import jax
import jax.numpy as jnp
from jax import lax
from jax.sharding import PartitionSpec as P

LOOP = 30
SPAN = 8192


def passed_along(value, axis, steps):
    count = lax.axis_size(axis)
    leading, last = (max(0, -steps), min(count, count - steps))
    return lax.ppermute(value, axis, [(source, source + steps) for source in range(leading, last)])


def shifted(value, axis, steps):
    count = lax.axis_size(axis)
    pairs = [(source, (source + steps) % count) for source in range(count)]
    return lax.ppermute(value, axis, pairs)


def band_matrix(weights, offset, width):
    source = jnp.arange(width + LOOP, dtype=jnp.int32)[:, None]
    target = jnp.arange(width, dtype=jnp.int32)[None, :]
    right_len = target + LOOP + 2 - offset - source
    inside = (right_len >= 1) & (right_len <= LOOP + 2 - offset)
    values = jnp.take(weights, jnp.clip(right_len - 1, 0, LOOP))
    return jnp.where(inside, values, jnp.zeros_like(values))


def on_device(
    sequence_codes,
    pair_allowed,
    stack_weight,
    hairpin_weight,
    loop_weight,
    inner_pairs,
    multi_left,
    branch_right,
):
    tile_count = lax.axis_size("tile")
    tile_id = lax.axis_index("tile")
    rep_id = lax.axis_index("rep")
    row_count = inner_pairs.shape[0]
    cols_local = pair_allowed.shape[1]
    rim_rows = passed_along(inner_pairs[: LOOP + 1], "tile", -1)
    extended = jnp.concatenate([inner_pairs, rim_rows], 0)
    first_col = rep_id * cols_local
    own_cols = lax.dynamic_slice_in_dim(extended, first_col, cols_local + LOOP, 1)
    bands = jnp.concatenate(
        [band_matrix(loop_weight[offset - 1], offset, cols_local) for offset in range(1, LOOP + 2)],
        1,
    )
    products = jnp.dot(own_cols, bands, precision=lax.Precision.HIGHEST)
    interior = jnp.zeros((row_count, cols_local), jnp.float32)
    for offset in range(1, LOOP + 2):
        interior = (
            interior
            + products[offset : offset + row_count, (offset - 1) * cols_local : offset * cols_local]
        )
    row_start = tile_id * row_count
    five_prime = lax.dynamic_slice_in_dim(sequence_codes, row_start, row_count, 0)
    segment = lax.dynamic_slice_in_dim(
        sequence_codes, row_start + SPAN + rep_id * cols_local, row_count + cols_local, 0
    )
    pair_index = (
        jnp.arange(row_count, dtype=jnp.int32)[:, None]
        + jnp.arange(cols_local, dtype=jnp.int32)[None, :]
    )
    three_prime = jnp.take(segment, pair_index)
    letters = jnp.arange(4, dtype=jnp.int32)
    onehot = (five_prime[:, None] == letters[None, :]).astype(jnp.float32)
    tables = jnp.dot(
        onehot, jnp.concatenate([stack_weight, hairpin_weight], 1), precision=lax.Precision.HIGHEST
    )
    stack_vals = jnp.zeros((row_count, cols_local), jnp.float32)
    hairpin_vals = jnp.zeros((row_count, cols_local), jnp.float32)
    for letter in range(4):
        matches = three_prime == letter
        stack_vals = stack_vals + jnp.where(matches, tables[:, letter][:, None], 0.0)
        hairpin_vals = hairpin_vals + jnp.where(matches, tables[:, 4 + letter][:, None], 0.0)
    paired_window = pair_allowed.astype(jnp.float32) * stack_vals * (hairpin_vals + interior)
    panels = branch_right[0]
    panel_count = panels.shape[0]
    arrived = [panels[0]]
    for distance in range(1, panel_count):
        hop_size = distance % tile_count
        arrived.append(shifted(panels[distance], "tile", -hop_size))
    arrived = jnp.stack(arrived, 0)
    split_local = multi_left.shape[2]
    local_row = jnp.arange(row_count, dtype=jnp.int32)[:, None]
    split_pos = rep_id * split_local + jnp.arange(split_local, dtype=jnp.int32)[None, :]
    first_panel = jnp.where(
        split_pos > local_row, multi_left[:, 0, :], jnp.zeros_like(multi_left[:, 0, :])
    )
    left_part = multi_left.at[:, 0, :].set(first_panel)
    partial_split = jnp.einsum("xmw,mwc->xc", left_part, arrived, precision=lax.Precision.HIGHEST)
    multi_split = lax.psum_scatter(partial_split, "rep", scatter_dimension=1, tiled=True)
    return (paired_window, multi_split)


def solution(mesh):
    placed = (
        P(),
        P("tile", "rep"),
        P(),
        P(),
        P(),
        P("tile", None),
        P("tile", None, "rep"),
        P("tile", None, "rep", None),
    )
    return jax.shard_map(
        on_device,
        mesh=mesh,
        in_specs=placed,
        out_specs=(P("tile", "rep"), P("tile", "rep")),
        check_vma=False,
    )
```

profile of v0, /device:TPU:56, one launch (start us, length us, event | category | flops | bytes accessed | tf_op | source)
XLA Modules:
  0.0 1085.1 jit_solution(67176634556041418)
XLA Ops:
  7.2 4.6 copy.63
  17.7 8.1 collective-permute-start.2
  74.5 20.2 %constant_dynamic-update-slice_fusion.30 = f32[158,3968]{1,0:T(8,128)S(1)} fusion(f32[]{:T(128)} %bitcast.41, f32[]{:T(128)} %bitcast.40, f32[]{:T(128)} %bitcast.39, f32[]{:T(128)} %bitcast.38, f32[]{:T(128)} %bitcast.37, f32[]{:T(128)} %bitcast.36, f32[]{:T(128)} %bitcast.35, f32[]{:T(128)} %bitcast.34, f32[]{:T(128)} %bitcast.33, f32[]{:T(128)} %bitcast.32, ...), kind=kLoop, calls=%fused_computation.144 | loop fusion | flops 1496575 | bytes 82556
  94.8 19.9 %constant_dynamic-update-slice_fusion.29 = f32[158,3968]{1,0:T(8,128)S(1)} fusion(f32[158,3968]{1,0:T(8,128)S(1)} %constant_dynamic-update-slice_fusion.30, f32[]{:T(128)} %bitcast.73, f32[]{:T(128)} %bitcast.72, f32[]{:T(128)} %bitcast.71, f32[]{:T(128)} %bitcast.70, f32[]{:T(128)} %bitcast.69, f32[]{:T(128)} %bitcast.68, f32[]{:T(128)} %bitcast.67, ...), kind=kLoop, calls=%fused_computation.143 | loop fusion | flops 1496576 | bytes 82556
  114.6 19.4 %constant_dynamic-update-slice_fusion.28 = f32[158,3968]{1,0:T(8,128)S(1)} fusion(f32[158,3968]{1,0:T(8,128)S(1)} %constant_dynamic-update-slice_fusion.29, f32[]{:T(128)} %bitcast.105, f32[]{:T(128)} %bitcast.104, f32[]{:T(128)} %bitcast.103, f32[]{:T(128)} %bitcast.102, f32[]{:T(128)} %bitcast.101, f32[]{:T(128)} %bitcast.100, f32[]{:T(128)} %bitcast.99, ...), kind=kLoop, calls=%fused_computation.142 | loop fusion | flops 1496576 | bytes 82556
  134.0 19.4 %constant_dynamic-update-slice_fusion.27 = f32[158,3968]{1,0:T(8,128)S(1)} fusion(f32[158,3968]{1,0:T(8,128)S(1)} %constant_dynamic-update-slice_fusion.28, f32[]{:T(128)} %bitcast.137, f32[]{:T(128)} %bitcast.136, f32[]{:T(128)} %bitcast.135, f32[]{:T(128)} %bitcast.134, f32[]{:T(128)} %bitcast.133, f32[]{:T(128)} %bitcast.132, f32[]{:T(128)} %bitcast.131, ...), kind=kLoop, calls=%fused_computation.141 | loop fusion | flops 1496576 | bytes 82556
  153.4 19.7 %constant_dynamic-update-slice_fusion.26 = f32[158,3968]{1,0:T(8,128)S(1)} fusion(f32[158,3968]{1,0:T(8,128)S(1)} %constant_dynamic-update-slice_fusion.27, f32[]{:T(128)} %bitcast.169, f32[]{:T(128)} %bitcast.168, f32[]{:T(128)} %bitcast.167, f32[]{:T(128)} %bitcast.166, f32[]{:T(128)} %bitcast.165, f32[]{:T(128)} %bitcast.164, f32[]{:T(128)} %bitcast.163, ...), kind=kLoop, calls=%fused_computation.140 | loop fusion | flops 1496576 | bytes 82556
  173.1 19.6 %constant_dynamic-update-slice_fusion.25 = f32[158,3968]{1,0:T(8,128)S(1)} fusion(f32[158,3968]{1,0:T(8,128)S(1)} %constant_dynamic-update-slice_fusion.26, f32[]{:T(128)} %bitcast.201, f32[]{:T(128)} %bitcast.200, f32[]{:T(128)} %bitcast.199, f32[]{:T(128)} %bitcast.198, f32[]{:T(128)} %bitcast.197, f32[]{:T(128)} %bitcast.196, f32[]{:T(128)} %bitcast.195, ...), kind=kLoop, calls=%fused_computation.139 | loop fusion | flops 1496576 | bytes 82556
  192.6 19.5 %constant_dynamic-update-slice_fusion.24 = f32[158,3968]{1,0:T(8,128)S(1)} fusion(f32[158,3968]{1,0:T(8,128)S(1)} %constant_dynamic-update-slice_fusion.25, f32[]{:T(128)} %bitcast.233, f32[]{:T(128)} %bitcast.232, f32[]{:T(128)} %bitcast.231, f32[]{:T(128)} %bitcast.230, f32[]{:T(128)} %bitcast.229, f32[]{:T(128)} %bitcast.228, f32[]{:T(128)} %bitcast.227, ...), kind=kLoop, calls=%fused_computation.138 | loop fusion | flops 1496576 | bytes 82556
  212.2 19.5 %constant_dynamic-update-slice_fusion.23 = f32[158,3968]{1,0:T(8,128)S(1)} fusion(f32[158,3968]{1,0:T(8,128)S(1)} %constant_dynamic-update-slice_fusion.24, f32[]{:T(128)} %bitcast.265, f32[]{:T(128)} %bitcast.264, f32[]{:T(128)} %bitcast.263, f32[]{:T(128)} %bitcast.262, f32[]{:T(128)} %bitcast.261, f32[]{:T(128)} %bitcast.260, f32[]{:T(128)} %bitcast.259, ...), kind=kLoop, calls=%fused_computation.137 | loop fusion | flops 1496576 | bytes 82556
  231.7 19.6 %constant_dynamic-update-slice_fusion.22 = f32[158,3968]{1,0:T(8,128)S(1)} fusion(f32[158,3968]{1,0:T(8,128)S(1)} %constant_dynamic-update-slice_fusion.23, f32[]{:T(128)} %bitcast.297, f32[]{:T(128)} %bitcast.296, f32[]{:T(128)} %bitcast.295, f32[]{:T(128)} %bitcast.294, f32[]{:T(128)} %bitcast.293, f32[]{:T(128)} %bitcast.292, f32[]{:T(128)} %bitcast.291, ...), kind=kLoop, calls=%fused_computation.136 | loop fusion | flops 1496576 | bytes 82556
  251.3 19.7 %constant_dynamic-update-slice_fusion.21 = f32[158,3968]{1,0:T(8,128)S(1)} fusion(f32[158,3968]{1,0:T(8,128)S(1)} %constant_dynamic-update-slice_fusion.22, f32[]{:T(128)} %bitcast.329, f32[]{:T(128)} %bitcast.328, f32[]{:T(128)} %bitcast.327, f32[]{:T(128)} %bitcast.326, f32[]{:T(128)} %bitcast.325, f32[]{:T(128)} %bitcast.324, f32[]{:T(128)} %bitcast.323, ...), kind=kLoop, calls=%fused_computation.135 | loop fusion | flops 1496576 | bytes 82556
  271.0 19.5 %constant_dynamic-update-slice_fusion.20 = f32[158,3968]{1,0:T(8,128)S(1)} fusion(f32[158,3968]{1,0:T(8,128)S(1)} %constant_dynamic-update-slice_fusion.21, f32[]{:T(128)} %bitcast.361, f32[]{:T(128)} %bitcast.360, f32[]{:T(128)} %bitcast.359, f32[]{:T(128)} %bitcast.358, f32[]{:T(128)} %bitcast.357, f32[]{:T(128)} %bitcast.356, f32[]{:T(128)} %bitcast.355, ...), kind=kLoop, calls=%fused_computation.134 | loop fusion | flops 1496576 | bytes 82556
  290.4 19.4 %constant_dynamic-update-slice_fusion.19 = f32[158,3968]{1,0:T(8,128)S(1)} fusion(f32[158,3968]{1,0:T(8,128)S(1)} %constant_dynamic-update-slice_fusion.20, f32[]{:T(128)} %bitcast.393, f32[]{:T(128)} %bitcast.392, f32[]{:T(128)} %bitcast.391, f32[]{:T(128)} %bitcast.390, f32[]{:T(128)} %bitcast.389, f32[]{:T(128)} %bitcast.388, f32[]{:T(128)} %bitcast.387, ...), kind=kLoop, calls=%fused_computation.133 | loop fusion | flops 1496576 | bytes 82556
  309.9 19.3 %constant_dynamic-update-slice_fusion.18 = f32[158,3968]{1,0:T(8,128)S(1)} fusion(f32[158,3968]{1,0:T(8,128)S(1)} %constant_dynamic-update-slice_fusion.19, f32[]{:T(128)} %bitcast.425, f32[]{:T(128)} %bitcast.424, f32[]{:T(128)} %bitcast.423, f32[]{:T(128)} %bitcast.422, f32[]{:T(128)} %bitcast.421, f32[]{:T(128)} %bitcast.420, f32[]{:T(128)} %bitcast.419, ...), kind=kLoop, calls=%fused_computation.132 | loop fusion | flops 1496576 | bytes 82556
  329.2 19.5 %constant_dynamic-update-slice_fusion.17 = f32[158,3968]{1,0:T(8,128)S(1)} fusion(f32[158,3968]{1,0:T(8,128)S(1)} %constant_dynamic-update-slice_fusion.18, f32[]{:T(128)} %bitcast.457, f32[]{:T(128)} %bitcast.456, f32[]{:T(128)} %bitcast.455, f32[]{:T(128)} %bitcast.454, f32[]{:T(128)} %bitcast.453, f32[]{:T(128)} %bitcast.452, f32[]{:T(128)} %bitcast.451, ...), kind=kLoop, calls=%fused_computation.131 | loop fusion | flops 1496576 | bytes 82556
  348.7 19.4 %constant_dynamic-update-slice_fusion.16 = f32[158,3968]{1,0:T(8,128)S(1)} fusion(f32[158,3968]{1,0:T(8,128)S(1)} %constant_dynamic-update-slice_fusion.17, f32[]{:T(128)} %bitcast.489, f32[]{:T(128)} %bitcast.488, f32[]{:T(128)} %bitcast.487, f32[]{:T(128)} %bitcast.486, f32[]{:T(128)} %bitcast.485, f32[]{:T(128)} %bitcast.484, f32[]{:T(128)} %bitcast.483, ...), kind=kLoop, calls=%fused_computation.130 | loop fusion | flops 1496576 | bytes 82556
  368.2 19.5 %constant_dynamic-update-slice_fusion.15 = f32[158,3968]{1,0:T(8,128)S(1)} fusion(f32[158,3968]{1,0:T(8,128)S(1)} %constant_dynamic-update-slice_fusion.16, f32[]{:T(128)} %bitcast.521, f32[]{:T(128)} %bitcast.520, f32[]{:T(128)} %bitcast.519, f32[]{:T(128)} %bitcast.518, f32[]{:T(128)} %bitcast.517, f32[]{:T(128)} %bitcast.516, f32[]{:T(128)} %bitcast.515, ...), kind=kLoop, calls=%fused_computation.129 | loop fusion | flops 1496576 | bytes 82556
  387.6 19.5 %constant_dynamic-update-slice_fusion.14 = f32[158,3968]{1,0:T(8,128)S(1)} fusion(f32[158,3968]{1,0:T(8,128)S(1)} %constant_dynamic-update-slice_fusion.15, f32[]{:T(128)} %bitcast.553, f32[]{:T(128)} %bitcast.552, f32[]{:T(128)} %bitcast.551, f32[]{:T(128)} %bitcast.550, f32[]{:T(128)} %bitcast.549, f32[]{:T(128)} %bitcast.548, f32[]{:T(128)} %bitcast.547, ...), kind=kLoop, calls=%fused_computation.128 | loop fusion | flops 1496576 | bytes 82556
  407.2 19.6 %constant_dynamic-update-slice_fusion.13 = f32[158,3968]{1,0:T(8,128)S(1)} fusion(f32[158,3968]{1,0:T(8,128)S(1)} %constant_dynamic-update-slice_fusion.14, f32[]{:T(128)} %bitcast.585, f32[]{:T(128)} %bitcast.584, f32[]{:T(128)} %bitcast.583, f32[]{:T(128)} %bitcast.582, f32[]{:T(128)} %bitcast.581, f32[]{:T(128)} %bitcast.580, f32[]{:T(128)} %bitcast.579, ...), kind=kLoop, calls=%fused_computation.127 | loop fusion | flops 1496576 | bytes 82556
  426.8 19.6 %constant_dynamic-update-slice_fusion.12 = f32[158,3968]{1,0:T(8,128)S(1)} fusion(f32[158,3968]{1,0:T(8,128)S(1)} %constant_dynamic-update-slice_fusion.13, f32[]{:T(128)} %bitcast.617, f32[]{:T(128)} %bitcast.616, f32[]{:T(128)} %bitcast.615, f32[]{:T(128)} %bitcast.614, f32[]{:T(128)} %bitcast.613, f32[]{:T(128)} %bitcast.612, f32[]{:T(128)} %bitcast.611, ...), kind=kLoop, calls=%fused_computation.126 | loop fusion | flops 1496576 | bytes 82556
  446.4 20.0 %constant_dynamic-update-slice_fusion.11 = f32[158,3968]{1,0:T(8,128)S(1)} fusion(f32[158,3968]{1,0:T(8,128)S(1)} %constant_dynamic-update-slice_fusion.12, f32[]{:T(128)} %bitcast.649, f32[]{:T(128)} %bitcast.648, f32[]{:T(128)} %bitcast.647, f32[]{:T(128)} %bitcast.646, f32[]{:T(128)} %bitcast.645, f32[]{:T(128)} %bitcast.644, f32[]{:T(128)} %bitcast.643, ...), kind=kLoop, calls=%fused_computation.125 | loop fusion | flops 1496576 | bytes 82556
  466.4 19.4 %constant_dynamic-update-slice_fusion.10 = f32[158,3968]{1,0:T(8,128)S(1)} fusion(f32[158,3968]{1,0:T(8,128)S(1)} %constant_dynamic-update-slice_fusion.11, f32[]{:T(128)} %bitcast.681, f32[]{:T(128)} %bitcast.680, f32[]{:T(128)} %bitcast.679, f32[]{:T(128)} %bitcast.678, f32[]{:T(128)} %bitcast.677, f32[]{:T(128)} %bitcast.676, f32[]{:T(128)} %bitcast.675, ...), kind=kLoop, calls=%fused_computation.124 | loop fusion | flops 1496576 | bytes 82556
  485.9 19.4 %constant_dynamic-update-slice_fusion.9 = f32[158,3968]{1,0:T(8,128)S(1)} fusion(f32[158,3968]{1,0:T(8,128)S(1)} %constant_dynamic-update-slice_fusion.10, f32[]{:T(128)} %bitcast.713, f32[]{:T(128)} %bitcast.712, f32[]{:T(128)} %bitcast.711, f32[]{:T(128)} %bitcast.710, f32[]{:T(128)} %bitcast.709, f32[]{:T(128)} %bitcast.708, f32[]{:T(128)} %bitcast.707, ...), kind=kLoop, calls=%fused_computation.123 | loop fusion | flops 1496576 | bytes 82556
  505.2 19.3 %constant_dynamic-update-slice_fusion.8 = f32[158,3968]{1,0:T(8,128)S(1)} fusion(f32[158,3968]{1,0:T(8,128)S(1)} %constant_dynamic-update-slice_fusion.9, f32[]{:T(128)} %bitcast.745, f32[]{:T(128)} %bitcast.744, f32[]{:T(128)} %bitcast.743, f32[]{:T(128)} %bitcast.742, f32[]{:T(128)} %bitcast.741, f32[]{:T(128)} %bitcast.740, f32[]{:T(128)} %bitcast.739, ...), kind=kLoop, calls=%fused_computation.122 | loop fusion | flops 1496576 | bytes 82556
  524.6 19.7 %constant_dynamic-update-slice_fusion.7 = f32[158,3968]{1,0:T(8,128)S(1)} fusion(f32[158,3968]{1,0:T(8,128)S(1)} %constant_dynamic-update-slice_fusion.8, f32[]{:T(128)} %bitcast.777, f32[]{:T(128)} %bitcast.776, f32[]{:T(128)} %bitcast.775, f32[]{:T(128)} %bitcast.774, f32[]{:T(128)} %bitcast.773, f32[]{:T(128)} %bitcast.772, f32[]{:T(128)} %bitcast.771, ...), kind=kLoop, calls=%fused_computation.121 | loop fusion | flops 1496576 | bytes 82556
  544.3 19.5 %constant_dynamic-update-slice_fusion.6 = f32[158,3968]{1,0:T(8,128)S(1)} fusion(f32[158,3968]{1,0:T(8,128)S(1)} %constant_dynamic-update-slice_fusion.7, f32[]{:T(128)} %bitcast.809, f32[]{:T(128)} %bitcast.808, f32[]{:T(128)} %bitcast.807, f32[]{:T(128)} %bitcast.806, f32[]{:T(128)} %bitcast.805, f32[]{:T(128)} %bitcast.804, f32[]{:T(128)} %bitcast.803, ...), kind=kLoop, calls=%fused_computation.120 | loop fusion | flops 1496576 | bytes 82556
  563.8 19.1 %constant_dynamic-update-slice_fusion.5 = f32[158,3968]{1,0:T(8,128)S(1)} fusion(f32[158,3968]{1,0:T(8,128)S(1)} %constant_dynamic-update-slice_fusion.6, f32[]{:T(128)} %bitcast.841, f32[]{:T(128)} %bitcast.840, f32[]{:T(128)} %bitcast.839, f32[]{:T(128)} %bitcast.838, f32[]{:T(128)} %bitcast.837, f32[]{:T(128)} %bitcast.836, f32[]{:T(128)} %bitcast.835, ...), kind=kLoop, calls=%fused_computation.119 | loop fusion | flops 1496576 | bytes 82556
  582.9 19.4 %constant_dynamic-update-slice_fusion.4 = f32[158,3968]{1,0:T(8,128)S(1)} fusion(f32[158,3968]{1,0:T(8,128)S(1)} %constant_dynamic-update-slice_fusion.5, f32[]{:T(128)} %bitcast.873, f32[]{:T(128)} %bitcast.872, f32[]{:T(128)} %bitcast.871, f32[]{:T(128)} %bitcast.870, f32[]{:T(128)} %bitcast.869, f32[]{:T(128)} %bitcast.868, f32[]{:T(128)} %bitcast.867, ...), kind=kLoop, calls=%fused_computation.118 | loop fusion | flops 1496576 | bytes 82556
  602.3 19.8 %constant_dynamic-update-slice_fusion.3 = f32[158,3968]{1,0:T(8,128)S(1)} fusion(f32[158,3968]{1,0:T(8,128)S(1)} %constant_dynamic-update-slice_fusion.4, f32[]{:T(128)} %bitcast.905, f32[]{:T(128)} %bitcast.904, f32[]{:T(128)} %bitcast.903, f32[]{:T(128)} %bitcast.902, f32[]{:T(128)} %bitcast.901, f32[]{:T(128)} %bitcast.900, f32[]{:T(128)} %bitcast.899, ...), kind=kLoop, calls=%fused_computation.117 | loop fusion | flops 1496576 | bytes 82556
  622.2 19.6 %constant_dynamic-update-slice_fusion.2 = f32[158,3968]{1,0:T(8,128)S(1)} fusion(f32[158,3968]{1,0:T(8,128)S(1)} %constant_dynamic-update-slice_fusion.3, f32[]{:T(128)} %bitcast.937, f32[]{:T(128)} %bitcast.936, f32[]{:T(128)} %bitcast.935, f32[]{:T(128)} %bitcast.934, f32[]{:T(128)} %bitcast.933, f32[]{:T(128)} %bitcast.932, f32[]{:T(128)} %bitcast.931, ...), kind=kLoop, calls=%fused_computation.116 | loop fusion | flops 1496576 | bytes 82556
  641.8 19.2 %constant_dynamic-update-slice_fusion.1 = f32[158,3968]{1,0:T(8,128)S(1)} fusion(f32[158,3968]{1,0:T(8,128)S(1)} %constant_dynamic-update-slice_fusion.2, f32[]{:T(128)} %bitcast.969, f32[]{:T(128)} %bitcast.968, f32[]{:T(128)} %bitcast.967, f32[]{:T(128)} %bitcast.966, f32[]{:T(128)} %bitcast.965, f32[]{:T(128)} %bitcast.964, f32[]{:T(128)} %bitcast.963, ...), kind=kLoop, calls=%fused_computation.115 | loop fusion | flops 1496576 | bytes 82556
  661.0 19.7 %constant_dynamic-update-slice_fusion = f32[158,3968]{1,0:T(8,128)S(1)} fusion(f32[158,3968]{1,0:T(8,128)S(1)} %constant_dynamic-update-slice_fusion.1, f32[]{:T(128)} %bitcast.1001, f32[]{:T(128)} %bitcast.1000, f32[]{:T(128)} %bitcast.999, f32[]{:T(128)} %bitcast.998, f32[]{:T(128)} %bitcast.997, f32[]{:T(128)} %bitcast.996, f32[]{:T(128)} %bitcast.995, ...), kind=kLoop, calls=%fused_computation.114 | loop fusion | flops 1496576 | bytes 82556 | tf_op jit(solution)/shard_map/concatenate | solution.py:50
  681.8 8.1 scatter.4
  691.9 5.3 collective-permute-start.6
  701.5 4.2 collective-permute-start.8
  707.3 6.8 collective-permute-start.9
  714.8 8.5 collective-permute-done.6
  723.3 7.0 collective-permute-start.10
  731.0 16.3 %collective-permute-done.7 = f32[128,512]{1,0:T(8,128)S(1)} collective-permute-done((f32[128,512]{1,0:T(8,128)}, f32[128,512]{1,0:T(8,128)S(1)}, u32[]{:S(2)}, u32[]{:S(2)}) %collective-permute-start.7) | collective-permute-done | bytes 262176 | tf_op jit(solution)/shard_map/ppermute | solution.py:19
  748.1 8.1 collective-permute-done.8
  760.9 5.8 collective-permute-done.11
  766.7 3.8 collective-permute-start.15
  771.3 7.0 collective-permute-done.12
  778.9 7.0 collective-permute-done.13
  793.9 11.3 %fusion.2 = f32[512,512]{1,0:T(8,128)} fusion(f32[16,128,512]{2,1,0:T(8,128)} %bitcast_dynamic-update-slice_fusion, f32[512,16,128]{2,1,0:T(8,128)S(1)} %copy-done), kind=kOutput, calls=%fused_computation.5 | convolution fusion | flops 6442450944 | bytes 9437184 | tf_op jit(solution)/shard_map/xmw,mwc->xc/dot_general | solution.py:97
  806.0 260.8 %gather_fusion = s32[65536]{0:T(1024)S(1)} fusion(s32[640]{0:T(1024)S(1)} %dynamic_slice.9, s32[65536]{0:T(1024)S(1)} %fusion.9), kind=kCustom, calls=%fused_computation | custom fusion | bytes 786432 | tf_op jit(solution)/shard_map/jit(_take)/gather | solution.py:70
  1066.9 8.8 fusion.6
  (166 shorter events, 82.9 us)
Async XLA Ops:
  7.2 1070.9 %reduce-scatter.2.cloned.1.call-start = ((), (), s32[]{:S(2)}) async-start(), calls=%async_computation.1 | async-start | bytes 1310720 | tf_op jit(solution)/shard_map/reduce_scatter | solution.py:98
  7.2 8.4 copy-start.1
  13.5 14.0 %copy-start.8 = (f32[31,31]{1,0:T(8,128)S(1)}, f32[31,31]{1,0:T(8,128)}, u32[]{:S(2)}) copy-start(f32[31,31]{1,0:T(8,128)} %param.16) | copy-start | bytes 11536
  13.5 1053.3 %collective-permute-start = (f32[31,542]{0,1:T(8,128)}, f32[31,542]{0,1:T(8,128)S(1)}, u32[]{:S(2)}, u32[]{:S(2)}) collective-permute-start(f32[31,542]{0,1:T(8,128)} %slice.310), channel_id=1, source_target_pairs={{4,0},{8,4},{12,8},{16,12},{20,16},{24,20},{28,24},{32,28},{36,32}... | collective-permute-start | bytes 201632 | tf_op jit(solution)/shard_map/ppermute | solution.py:13
  17.5 672.4 %collective-permute-start.1 = (f32[128,512]{1,0:T(8,128)}, f32[128,512]{1,0:T(8,128)}, u32[]{:S(2)}, u32[]{:S(2)}) collective-permute-start(f32[128,512]{1,0:T(8,128)} %get-tuple-element.28), channel_id=1, source_target_pairs={{0,252},{4,0},{8,4},{12,8},{16,12},{20,16},{24,20},{28,24},{32,28}... | collective-permute-start | bytes 786440 | tf_op jit(solution)/shard_map/ppermute | solution.py:19
  17.7 674.2 %collective-permute-start.2 = (f32[128,512]{1,0:T(8,128)}, f32[128,512]{1,0:T(8,128)}, u32[]{:S(2)}, u32[]{:S(2)}) collective-permute-start(f32[128,512]{1,0:T(8,128)} %get-tuple-element.27), channel_id=1, source_target_pairs={{0,248},{4,252},{8,0},{12,4},{16,8},{20,12},{24,16},{28,20},{32,24... | collective-permute-start | bytes 786440 | tf_op jit(solution)/shard_map/ppermute | solution.py:19
  25.7 673.2 %collective-permute-start.3 = (f32[128,512]{1,0:T(8,128)}, f32[128,512]{1,0:T(8,128)}, u32[]{:S(2)}, u32[]{:S(2)}) collective-permute-start(f32[128,512]{1,0:T(8,128)} %get-tuple-element.26), channel_id=1, source_target_pairs={{0,244},{4,248},{8,252},{12,0},{16,4},{20,8},{24,12},{28,16},{32,2... | collective-permute-start | bytes 786440 | tf_op jit(solution)/shard_map/ppermute | solution.py:19
  26.3 675.1 %collective-permute-start.4 = (f32[128,512]{1,0:T(8,128)}, f32[128,512]{1,0:T(8,128)}, u32[]{:S(2)}, u32[]{:S(2)}) collective-permute-start(f32[128,512]{1,0:T(8,128)} %get-tuple-element.25), channel_id=1, source_target_pairs={{0,240},{4,244},{8,248},{12,252},{16,0},{20,4},{24,8},{28,12},{32,... | collective-permute-start | bytes 786440 | tf_op jit(solution)/shard_map/ppermute | solution.py:19
  231.7 449.8 %copy-start.9 = (f32[4,4]{1,0:T(4,128)S(1)}, f32[4,4]{1,0:T(4,128)}, u32[]{:S(2)}) copy-start(f32[4,4]{1,0:T(4,128)} %param.15) | copy-start | bytes 196
  231.7 449.8 %copy-start.10 = (f32[4,4]{1,0:T(4,128)S(1)}, f32[4,4]{1,0:T(4,128)}, u32[]{:S(2)}) copy-start(f32[4,4]{1,0:T(4,128)} %param.14) | copy-start | bytes 196
  689.9 33.4 %copy-start.7 = (f32[128,512]{1,0:T(8,128)S(1)}, f32[128,512]{1,0:T(8,128)}, u32[]{:S(2)}) copy-start(f32[128,512]{1,0:T(8,128)} %get-tuple-element.19) | copy-start | bytes 786436
  689.9 57.5 %copy-start.6 = (f32[128,512]{1,0:T(8,128)S(1)}, f32[128,512]{1,0:T(8,128)}, u32[]{:S(2)}) copy-start(f32[128,512]{1,0:T(8,128)} %get-tuple-element.18) | copy-start | bytes 786436
  689.9 66.3 %copy-start.5 = (f32[128,512]{1,0:T(8,128)S(1)}, f32[128,512]{1,0:T(8,128)}, u32[]{:S(2)}) copy-start(f32[128,512]{1,0:T(8,128)} %get-tuple-element.17) | copy-start | bytes 786436
  689.9 69.1 %copy-start.4 = (f32[128,512]{1,0:T(8,128)S(1)}, f32[128,512]{1,0:T(8,128)}, u32[]{:S(2)}) copy-start(f32[128,512]{1,0:T(8,128)} %get-tuple-element.16) | copy-start | bytes 786436
  689.9 70.3 %copy-start.3 = (f32[128,512]{1,0:T(8,128)S(1)}, f32[128,512]{1,0:T(8,128)}, u32[]{:S(2)}) copy-start(f32[128,512]{1,0:T(8,128)} %get-tuple-element.29) | copy-start | bytes 786436
  689.9 17.4 %collective-permute-start.5 = (f32[128,512]{1,0:T(8,128)}, f32[128,512]{1,0:T(8,128)S(1)}, u32[]{:S(2)}, u32[]{:S(2)}) collective-permute-start(f32[128,512]{1,0:T(8,128)} %get-tuple-element.24), channel_id=1, source_target_pairs={{0,236},{4,240},{8,244},{12,248},{16,252},{20,0},{24,4},{28,8},{32... | collective-permute-start | bytes 786440 | tf_op jit(solution)/shard_map/ppermute | solution.py:19
  691.9 31.4 %collective-permute-start.6 = (f32[128,512]{1,0:T(8,128)}, f32[128,512]{1,0:T(8,128)S(1)}, u32[]{:S(2)}, u32[]{:S(2)}) collective-permute-start(f32[128,512]{1,0:T(8,128)} %get-tuple-element.23), channel_id=1, source_target_pairs={{0,232},{4,236},{8,240},{12,244},{16,248},{20,252},{24,0},{28,4},{... | collective-permute-start | bytes 786440 | tf_op jit(solution)/shard_map/ppermute | solution.py:19
  698.9 48.5 %collective-permute-start.7 = (f32[128,512]{1,0:T(8,128)}, f32[128,512]{1,0:T(8,128)S(1)}, u32[]{:S(2)}, u32[]{:S(2)}) collective-permute-start(f32[128,512]{1,0:T(8,128)} %get-tuple-element.22), channel_id=1, source_target_pairs={{0,228},{4,232},{8,236},{12,240},{16,244},{20,248},{24,252},{28,0}... | collective-permute-start | bytes 786440 | tf_op jit(solution)/shard_map/ppermute | solution.py:19
  701.5 54.7 %collective-permute-start.8 = (f32[128,512]{1,0:T(8,128)}, f32[128,512]{1,0:T(8,128)S(1)}, u32[]{:S(2)}, u32[]{:S(2)}) collective-permute-start(f32[128,512]{1,0:T(8,128)} %get-tuple-element.21), channel_id=1, source_target_pairs={{0,224},{4,228},{8,232},{12,236},{16,240},{20,244},{24,248},{28,25... | collective-permute-start | bytes 786440 | tf_op jit(solution)/shard_map/ppermute | solution.py:19
  707.3 51.7 %collective-permute-start.9 = (f32[128,512]{1,0:T(8,128)}, f32[128,512]{1,0:T(8,128)S(1)}, u32[]{:S(2)}, u32[]{:S(2)}) collective-permute-start(f32[128,512]{1,0:T(8,128)} %get-tuple-element.20), channel_id=1, source_target_pairs={{0,220},{4,224},{8,228},{12,232},{16,236},{20,240},{24,244},{28,24... | collective-permute-start | bytes 786440 | tf_op jit(solution)/shard_map/ppermute | solution.py:19
  723.3 70.5 %copy-start = (f32[512,16,128]{2,1,0:T(8,128)S(1)}, f32[512,16,128]{2,1,0:T(8,128)}, u32[]{:S(2)}) copy-start(f32[512,16,128]{2,1,0:T(8,128)} %scatter.4) | copy-start | bytes 12582916
  723.3 36.8 %collective-permute-start.10 = (f32[128,512]{1,0:T(8,128)S(1)}, f32[128,512]{1,0:T(8,128)S(1)}, u32[]{:S(2)}, u32[]{:S(2)}) collective-permute-start(f32[128,512]{1,0:T(8,128)S(1)} %copy-done.7), channel_id=1, source_target_pairs={{0,216},{4,220},{8,224},{12,228},{16,232},{20,236},{24,240},{28,24... | collective-permute-start | bytes 786440 | tf_op jit(solution)/shard_map/ppermute | solution.py:19
  747.4 19.3 %collective-permute-start.11 = (f32[128,512]{1,0:T(8,128)S(1)}, f32[128,512]{1,0:T(8,128)S(1)}, u32[]{:S(2)}, u32[]{:S(2)}) collective-permute-start(f32[128,512]{1,0:T(8,128)S(1)} %copy-done.6), channel_id=1, source_target_pairs={{0,212},{4,216},{8,220},{12,224},{16,228},{20,232},{24,236},{28,24... | collective-permute-start | bytes 786440 | tf_op jit(solution)/shard_map/ppermute | solution.py:19
  756.1 22.1 %collective-permute-start.12 = (f32[128,512]{1,0:T(8,128)S(1)}, f32[128,512]{1,0:T(8,128)S(1)}, u32[]{:S(2)}, u32[]{:S(2)}) collective-permute-start(f32[128,512]{1,0:T(8,128)S(1)} %copy-done.5), channel_id=1, source_target_pairs={{0,208},{4,212},{8,216},{12,220},{16,224},{20,228},{24,232},{28,23... | collective-permute-start | bytes 786440 | tf_op jit(solution)/shard_map/ppermute | solution.py:19
  759.0 26.9 %collective-permute-start.13 = (f32[128,512]{1,0:T(8,128)S(1)}, f32[128,512]{1,0:T(8,128)S(1)}, u32[]{:S(2)}, u32[]{:S(2)}) collective-permute-start(f32[128,512]{1,0:T(8,128)S(1)} %copy-done.4), channel_id=1, source_target_pairs={{0,204},{4,208},{8,212},{12,216},{16,220},{20,224},{24,228},{28,23... | collective-permute-start | bytes 786440 | tf_op jit(solution)/shard_map/ppermute | solution.py:19
  760.1 30.1 %collective-permute-start.14 = (f32[128,512]{1,0:T(8,128)S(1)}, f32[128,512]{1,0:T(8,128)S(1)}, u32[]{:S(2)}, u32[]{:S(2)}) collective-permute-start(f32[128,512]{1,0:T(8,128)S(1)} %copy-done.3), channel_id=1, source_target_pairs={{0,200},{4,204},{8,208},{12,212},{16,216},{20,220},{24,224},{28,22... | collective-permute-start | bytes 786440 | tf_op jit(solution)/shard_map/ppermute | solution.py:19
  766.7 26.4 %collective-permute-start.15 = (f32[128,512]{1,0:T(8,128)S(1)}, f32[128,512]{1,0:T(8,128)S(1)}, u32[]{:S(2)}, u32[]{:S(2)}) collective-permute-start(f32[128,512]{1,0:T(8,128)S(1)} %get-tuple-element.15), channel_id=1, source_target_pairs={{0,196},{4,200},{8,204},{12,208},{16,212},{20,216},{24,220},{28,22... | collective-permute-start | bytes 786440 | tf_op jit(solution)/shard_map/ppermute | solution.py:19
  1066.8 8.8 copy-start.2
Sparse Core Ops, SparseCore 0:
  805.3 24.8 reduce-scatter.1
where the time goes:
time: 1100 us; the launch traced here: 1090 us
  other arithmetic  610 us (55%)
  local copies, waits for them, and re-layouts  338 us (31%)
  waiting for transfers between devices  58.4 us (5%)
  starting transfers between devices  42.8 us (4%)
  matrix products  20.4 us (2%)
  between operations  14.8 us (1%)
    unnamed x30, other arithmetic  586 us
    gather x1, local copies, waits for them, and re-layouts, on_device(): three_prime = jnp.take(segment, pair_index)  261 us
    ppermute x15, waiting for transfers between devices, shifted(): return lax.ppermute(value, axis, pairs)  58.4 us
    gather x62, local copies, waits for them, and re-layouts, band_matrix(): values = jnp.take(weights, jnp.clip(right_len - 1, 0, LOOP))  44.2 us
    ppermute x15, starting transfers between devices, shifted(): return lax.ppermute(value, axis, pairs)  40.8 us
  transfers between devices with their start and end apart: 17, of which 8 were waited for; matrix products, arithmetic and copies ran while one was open for 89% of the time, Pallas kernels for 0%

commit v1 on v0

v1 whole, which is shorter than its diff:
```python
import functools

import jax
import jax.numpy as jnp
from jax import lax
from jax.experimental import pallas as pl
from jax.experimental.pallas import tpu as pltpu
from jax.sharding import PartitionSpec as P

LOOP = 30
SPAN = 8192
LANES = 128
RIM = 32
MESH = pl.DeviceIdType.MESH
F32 = jnp.float32
BF16 = jnp.bfloat16
BLOCK_ORDER = (2, 1, 3, 0)


def halves(value):
    high = value.astype(BF16)
    return high, (value - high.astype(F32)).astype(BF16)


def dot(left, right):
    return jnp.dot(left, right, preferred_element_type=F32)


def product(left_high, left_low, right):
    right_high, right_low = halves(right)
    width = right.shape[1]
    both = dot(left_high, jnp.concatenate([right_high, right_low], 1))
    return both[:, :width] + both[:, width:] + dot(left_low, right_high)


def kernel(
    tiles,
    reps,
    stack_ref,
    hairpin_ref,
    loop_ref,
    codes_hbm,
    allowed_hbm,
    inner_hbm,
    left_hbm,
    right_hbm,
    paired_hbm,
    split_hbm,
    codes,
    allowed,
    inner,
    rows,
    moving,
    weights,
    interior,
    left,
    left_high,
    left_low,
    panels,
    sums,
    others,
    local_sem,
    panel_send,
    panel_recv,
    rim_send,
    rim_recv,
    sum_send,
    sum_recv,
):
    tile = lax.axis_index("tile")
    rep = lax.axis_index("rep")
    panel_count, depth, _ = panels.shape
    row_count = rows.shape[0] - RIM

    def tile_at(step):
        return lax.rem(tile + step + tiles, tiles)

    def rep_at(step):
        return lax.rem(rep + step + reps, reps)

    barrier = pltpu.get_barrier_semaphore()

    @pl.loop(1, panel_count)
    def _(distance):
        pl.semaphore_signal(
            barrier, inc=1, device_id={"tile": tile_at(distance)}, device_id_type=MESH
        )

    for step in range(1, reps):
        pl.semaphore_signal(barrier, inc=1, device_id={"rep": rep_at(step)}, device_id_type=MESH)

    fetch_inner = pltpu.make_async_copy(inner_hbm, inner, local_sem.at[0])
    fetch_left = pltpu.make_async_copy(left_hbm, left, local_sem.at[1])
    fetch_right = pltpu.make_async_copy(right_hbm.at[0], panels.at[0], local_sem.at[2])
    fetch_codes = pltpu.make_async_copy(codes_hbm, codes, local_sem.at[3])
    fetch_allowed = pltpu.make_async_copy(allowed_hbm, allowed, local_sem.at[4])
    fetch_inner.start()
    fetch_left.start()
    fetch_right.start()
    fetch_codes.start()
    fetch_allowed.start()
    pl.semaphore_wait(barrier, panel_count - 1 + reps - 1)

    def columns(block):
        start = rep_at(BLOCK_ORDER[block]) * LANES
        return pl.ds(pl.multiple_of(start, LANES), LANES)

    def panel_copy(distance, block):
        place = (distance, slice(None), columns(block))
        return pltpu.make_async_remote_copy(
            src_ref=right_hbm.at[place],
            dst_ref=panels.at[place],
            send_sem=panel_send.at[distance, block],
            recv_sem=panel_recv.at[distance, block],
            device_id={"tile": tile_at(-distance)},
            device_id_type=MESH,
        )

    def send_block(block):
        @pl.loop(1, panel_count)
        def _(distance):
            panel_copy(distance, block).start()

    send_block(0)

    fetch_inner.wait()
    main_part = inner[pl.ds(pl.multiple_of(rep * LANES, LANES), LANES), :]
    rows[0:row_count, 0:LANES] = main_part.T
    tail_part = inner[pl.ds(pl.multiple_of((rep + 1) * LANES - 8, 8), LOOP + 8), :]
    rows[0:row_count, LANES : 2 * LANES] = jnp.zeros((row_count, LANES), F32)
    rows[0:row_count, LANES : LANES + LOOP + 8] = tail_part.T

    fetch_left.wait()
    own_row = lax.broadcasted_iota(jnp.int32, (row_count, LANES), 0)
    own_lane = lax.broadcasted_iota(jnp.int32, (row_count, LANES), 1)
    for panel in range(panel_count):
        value = left[pl.ds(panel, row_count, stride=panel_count), :]
        if panel == 0:
            value = jnp.where(own_lane + rep * LANES > own_row, value, 0.0)
        high, low = halves(value)
        at = slice((panel % 2) * LANES, (panel % 2 + 1) * LANES)
        left_high[panel // 2, :, at] = high
        left_low[panel // 2, :, at] = low

    rim_copy = pltpu.make_async_remote_copy(
        src_ref=rows.at[0:RIM],
        dst_ref=rows.at[row_count : row_count + RIM],
        send_sem=rim_send,
        recv_sem=rim_recv,
        device_id={"tile": tile_at(-1)},
        device_id_type=MESH,
    )
    rim_copy.start()
    for block in range(1, reps):
        send_block(block)
    fetch_right.wait()

    def add_pair(block, pair):
        @pl.when(pair > 0)
        def _():
            panel_copy(2 * pair, block).wait_recv()

        panel_copy(2 * pair + 1, block).wait_recv()
        right = panels[pl.ds(2 * pair, 2), :, columns(block)].reshape(2 * depth, LANES)
        value = product(left_high[pair], left_low[pair], right)

        @pl.when(pair == 0)
        def _():
            sums[block] = value

        @pl.when(pair > 0)
        def _():
            sums[block] += value

    def sum_copy(block):
        step = BLOCK_ORDER[block]
        return pltpu.make_async_remote_copy(
            src_ref=sums.at[block],
            dst_ref=others.at[block],
            send_sem=sum_send.at[block],
            recv_sem=sum_recv.at[block],
            device_id={"rep": rep_at(step)},
            device_id_type=MESH,
        )

    def work_block(block, first):
        @pl.loop(first, panel_count // 2)
        def _(pair):
            add_pair(block, pair)

    work_block(0, 0)

    rim_copy.wait_recv()

    @pl.when(tile == tiles - 1)
    def _():
        rows[row_count : row_count + RIM, :] = jnp.zeros((RIM, 2 * LANES), F32)

    sum_copy(0).start()
    weights[...] = jnp.zeros_like(weights)
    weights[0 : LOOP + 1, 0 : LOOP + 1] = loop_ref[...]
    interior[...] = jnp.zeros_like(interior)

    moving[...] = rows[...]

    def staircase(row, direction):
        width = row.shape[1]
        step = jnp.broadcast_to(row, (8, width))
        down = lax.broadcasted_iota(jnp.int32, (8, width), 0)
        for bit in (1, 2, 4):
            step = jnp.where(down & bit != 0, pltpu.roll(step, (direction * bit) % width, 1), step)
        return step

    tall = (LANES + 40, LANES)
    source = lax.broadcasted_iota(jnp.int32, tall, 0)
    source = jnp.where(source < LANES, source, source - 8)
    behind = source - lax.broadcasted_iota(jnp.int32, tall, 1)
    behind = jnp.where(lax.broadcasted_iota(jnp.int32, tall, 0) // 8 == LANES // 8, -1, behind)
    groups = [group % 16 for group in (*range(16), *range(15, 20))]

    @pl.loop(1, LOOP + 2)
    def _(offset):
        row = pltpu.roll(weights[pl.ds(offset - 1, 1), :], LANES - LOOP - 1 + offset, 1)
        step = staircase(row, 1)
        bands = jnp.concatenate([pltpu.roll(step, 8 * group, 1) for group in groups], 0)
        bands = jnp.where((behind >= 0) & (behind <= LOOP + 1 - offset), bands, 0.0)
        bands = jnp.concatenate([bands, jnp.zeros((LANES - 40, LANES), F32)], 0)
        later = moving[1 : row_count + RIM, :]
        moving[0 : row_count + RIM - 1, :] = later
        high, low = halves(later[0:row_count])
        interior[...] += product(high, low, bands)

    fetch_codes.wait()
    fetch_allowed.wait()
    row_blocks = row_count // LANES
    square = (LANES, LANES)
    down = lax.broadcasted_iota(jnp.int32, square, 0)
    across = lax.broadcasted_iota(jnp.int32, square, 1)
    ones = jnp.ones(square, BF16)
    code_row = tile * row_blocks
    for part in range(row_blocks):
        five = codes[pl.ds(code_row + part, 1), :]
        five = jnp.where(down == across, jnp.broadcast_to(five, square), 0).astype(F32)
        three_row = code_row + SPAN // LANES + rep + part
        three = jnp.concatenate(
            [codes[pl.ds(three_row, 1), :], codes[pl.ds(three_row + 1, 1), :]], 1
        ).astype(F32)
        step = staircase(three, -1)
        three = jnp.concatenate(
            [pltpu.roll(step, (-8 * group) % (2 * LANES), 1)[:, :LANES] for group in range(16)], 0
        )
        code = dot((4.0 * five).astype(BF16), ones) + three
        stack_value = jnp.zeros(square, F32)
        hairpin_value = jnp.zeros(square, F32)
        for first in range(4):
            for second in range(4):
                match = code == float(4 * first + second)
                stack_value = jnp.where(match, stack_ref[first, second], stack_value)
                hairpin_value = jnp.where(match, hairpin_ref[first, second], hairpin_value)
        at = slice(part * LANES, (part + 1) * LANES)
        interior[at] = (allowed[at].astype(F32) * stack_value) * (hairpin_value + interior[at])

    for block in range(1, reps):
        work_block(block, 0) if block < reps - 1 else None
        if block == 1:
            store_paired = pltpu.make_async_copy(interior, paired_hbm, local_sem.at[5])
            store_paired.start()
        if block < reps - 1:
            sum_copy(block).start()
    work_block(reps - 1, 0)

    for block in range(reps - 1):
        sum_copy(block).wait_recv()
    sums[reps - 1] = (sums[reps - 1] + others[0]) + (others[1] + others[2])
    store_split = pltpu.make_async_copy(sums.at[reps - 1], split_hbm, local_sem.at[6])
    store_split.start()
    store_paired.wait()
    store_split.wait()
    rim_copy.wait_send()
    for block in range(reps):

        @pl.loop(1, panel_count)
        def _(distance):
            panel_copy(distance, block).wait_send()

        if block < reps - 1:
            sum_copy(block).wait_send()


def on_device(
    tiles,
    reps,
    sequence_codes,
    pair_allowed,
    stack_weight,
    hairpin_weight,
    loop_weight,
    inner_pairs,
    multi_left,
    branch_right,
):
    row_count, cols_local = pair_allowed.shape
    panel_count = multi_left.shape[1]
    codes = sequence_codes.reshape(-1, LANES)
    inner = inner_pairs.T
    left = multi_left.reshape(row_count * panel_count, cols_local)
    right = branch_right[0]
    out = jax.ShapeDtypeStruct((row_count, cols_local), F32)
    any_space = pl.BlockSpec(memory_space=pl.ANY)
    smem = pl.BlockSpec(memory_space=pltpu.SMEM)
    vmem = pl.BlockSpec(memory_space=pltpu.VMEM)
    block = (row_count, LANES)
    pairs = (panel_count // 2, row_count, 2 * LANES)
    dma = pltpu.SemaphoreType.DMA
    return pl.pallas_call(
        functools.partial(kernel, tiles, reps),
        out_shape=(out, out),
        in_specs=[smem, smem, vmem] + [any_space] * 5,
        out_specs=(any_space, any_space),
        scratch_shapes=[
            pltpu.VMEM(codes.shape, jnp.int32),
            pltpu.VMEM(block, jnp.int32),
            pltpu.VMEM(inner.shape, F32),
            pltpu.VMEM((row_count + RIM, 2 * LANES), F32),
            pltpu.VMEM((row_count + RIM, 2 * LANES), F32),
            pltpu.VMEM((32, LANES), F32),
            pltpu.VMEM(block, F32),
            pltpu.VMEM(left.shape, F32),
            pltpu.VMEM(pairs, BF16),
            pltpu.VMEM(pairs, BF16),
            pltpu.VMEM(right.shape, F32),
            pltpu.VMEM((reps,) + block, F32),
            pltpu.VMEM((reps - 1,) + block, F32),
            dma((7,)),
            dma((panel_count, reps)),
            dma((panel_count, reps)),
            dma,
            dma,
            dma((reps - 1,)),
            dma((reps - 1,)),
        ],
        compiler_params=pltpu.CompilerParams(
            collective_id=0, has_side_effects=True, vmem_limit_bytes=60 << 20
        ),
    )(stack_weight, hairpin_weight, loop_weight, codes, pair_allowed, inner, left, right)


def solution(mesh):
    placed = (
        P(),
        P("tile", "rep"),
        P(),
        P(),
        P(),
        P("tile", None),
        P("tile", None, "rep"),
        P("tile", None, "rep", None),
    )
    return jax.shard_map(
        functools.partial(on_device, mesh.shape["tile"], mesh.shape["rep"]),
        mesh=mesh,
        in_specs=placed,
        out_specs=(P("tile", "rep"), P("tile", "rep")),
        check_vma=False,
    )
```

time: 1100 us -> 111 us (0.10); the launches traced: 1090 us -> 110 us
  other arithmetic: 610 us -> 0 us
  local copies, waits for them, and re-layouts: 338 us -> 3.34 us
  Pallas kernels: 0 us -> 106 us
  waiting for transfers between devices: 58.4 us -> 0 us
  starting transfers between devices: 42.8 us -> 0 us
  matrix products: 20.4 us -> 0 us
  between operations: 14.8 us -> 0.64 us
    unnamed x30 -> x0, other arithmetic: 586 us -> none
    gather x63 -> x0, local copies, waits for them, and re-layouts: 305 us -> none  [the longest x1 261 us: on_device(): three_prime = jnp.take(segment, pair_index)]
    pallas_call x0 -> x1, Pallas kernels: none -> 106 us  [on_device(): pl.pallas_call(functools.partial(kernel, tiles, reps), out_shape=(out, ou...]
    ppermute x16 -> x0, waiting for transfers between devices: 58.4 us -> none  [the longest x15 58.4 us: shifted(): return lax.ppermute(value, axis, pairs)]
    ppermute x16 -> x0, starting transfers between devices: 42.8 us -> none  [the longest x15 40.8 us: shifted(): return lax.ppermute(value, axis, pairs)]
    dot_general x3 -> x0, matrix products: 20.4 us -> none  [the longest x1 11.3 us: on_device(): jnp.einsum('xmw,mwc->xc', left_part, arrived, precision=lax.Precision.HIG...]
    concatenate x1 -> x0, other arithmetic: 19.7 us -> none  [on_device(): jnp.concatenate([band_matrix(loop_weight[offset - 1], offset, cols_local)...]
    unnamed x38 -> x2, local copies, waits for them, and re-layouts: 19.5 us -> 3.34 us
  transfers between devices with their start and end apart: 17 -> 0, of which waited for: 8 -> 0; matrix products, arithmetic and copies ran while one was open for 89% -> 0% of each run, Pallas kernels for 0% -> 0%
where the time goes in v1:
time: 111 us; the launch traced here: 110 us
  Pallas kernels  106 us (95%)
  local copies, waits for them, and re-layouts  3.34 us (3%)
    pallas_call x1, Pallas kernels, on_device(): pl.pallas_call(functools.partial(kernel, tiles, reps), out_shape=(out, ou...  106 us
    unnamed x2, local copies, waits for them, and re-layouts  3.34 us

profile of v1, /device:TPU:56, one launch (start us, length us, event | category | flops | bytes accessed | tf_op | source)
XLA Modules:
  0.0 110.2 jit_solution(14502013548319428256)
XLA Ops:
  0.6 106.2 %shard_map.95 = (f32[512,128]{1,0:T(8,128)}, f32[512,128]{1,0:T(8,128)}) custom-call(f32[4,4]{1,0:T(4,128)} %stack_ref.1, f32[4,4]{1,0:T(4,128)} %hairpin_ref.1, f32[31,31]{1,0:T(8,128)} %loop_ref.1, s32[324,128]{1,0:T(8,128)} %bitcast.7, s32[512,128]{1,0:T(8,128)} %allowed_hbm.1, f32[542,512]{1,0:T(8,128)} %bitcast.6, f32[8192,128]{1,0:T(8,128)} %bitcast.4, ...), custom_call_target="tpu_custom_call" | custom-call | tf_op jit(solution)/shard_map/pallas_call | solution.py:315
  106.8 1.7 %copy.12 = f32[512,128]{1,0:T(8,128)} copy(f32[512,128]{1,0:T(8,128)} %get-tuple-element.4) | data formatting | bytes 524288
  108.5 1.7 %copy.13 = f32[512,128]{1,0:T(8,128)} copy(f32[512,128]{1,0:T(8,128)} %get-tuple-element.5) | data formatting | bytes 524288

commit v2 on v1

--- a/solution.py
+++ b/solution.py
@@ -15,6 +15,7 @@
 F32 = jnp.float32
 BF16 = jnp.bfloat16
 BLOCK_ORDER = (2, 1, 3, 0)
+SEND_ORDER = (2, 14, 4, 12, 6, 10, 8, 1, 15, 3, 13, 5, 11, 7, 9)
 
 
 def halves(value):
@@ -110,15 +111,14 @@
         return pltpu.make_async_remote_copy(
             src_ref=right_hbm.at[place],
             dst_ref=panels.at[place],
-            send_sem=panel_send.at[distance, block],
-            recv_sem=panel_recv.at[distance, block],
+            send_sem=panel_send,
+            recv_sem=panel_recv.at[distance // 2, block],
             device_id={"tile": tile_at(-distance)},
             device_id_type=MESH,
         )
 
     def send_block(block):
-        @pl.loop(1, panel_count)
-        def _(distance):
+        for distance in SEND_ORDER if block < reps - 1 else range(1, panel_count):
             panel_copy(distance, block).start()
 
     send_block(0)
@@ -155,12 +155,19 @@
         send_block(block)
     fetch_right.wait()
 
+    def wait_for(first, count, place, sem):
+        ref = panels.at[pl.ds(first, count), :, place]
+        pltpu.make_async_copy(ref, ref, sem).wait()
+
     def add_pair(block, pair):
         @pl.when(pair > 0)
         def _():
-            panel_copy(2 * pair, block).wait_recv()
-
-        panel_copy(2 * pair + 1, block).wait_recv()
+            wait_for(2 * pair, 2, columns(block), panel_recv.at[pair, block])
+
+        @pl.when(pair == 0)
+        def _():
+            wait_for(1, 1, columns(block), panel_recv.at[pair, block])
+
         right = panels[pl.ds(2 * pair, 2), :, columns(block)].reshape(2 * depth, LANES)
         value = product(left_high[pair], left_low[pair], right)
 
@@ -177,7 +184,7 @@
         return pltpu.make_async_remote_copy(
             src_ref=sums.at[block],
             dst_ref=others.at[block],
-            send_sem=sum_send.at[block],
+            send_sem=sum_send,
             recv_sem=sum_recv.at[block],
             device_id={"rep": rep_at(step)},
             device_id_type=MESH,
@@ -277,14 +284,9 @@
     store_paired.wait()
     store_split.wait()
     rim_copy.wait_send()
-    for block in range(reps):
-
-        @pl.loop(1, panel_count)
-        def _(distance):
-            panel_copy(distance, block).wait_send()
-
-        if block < reps - 1:
-            sum_copy(block).wait_send()
+    wait_for(1, panel_count - 1, slice(None), panel_send)
+    sent = sums.at[0 : reps - 1]
+    pltpu.make_async_copy(sent, sent, sum_send).wait()
 
 
 def on_device(
@@ -332,11 +334,11 @@
             pltpu.VMEM((reps,) + block, F32),
             pltpu.VMEM((reps - 1,) + block, F32),
             dma((7,)),
-            dma((panel_count, reps)),
-            dma((panel_count, reps)),
+            dma,
+            dma((panel_count // 2, reps)),
             dma,
             dma,
-            dma((reps - 1,)),
+            dma,
             dma((reps - 1,)),
         ],
         compiler_params=pltpu.CompilerParams(

time: 111 us -> 109 us (0.982)
    pallas_call x1, Pallas kernels: 106 us -> 105 us  [on_device(): pl.pallas_call(functools.partial(kernel, tiles, reps), out_shape=(out, ou...]
where the time goes in v2:
time: 109 us
  Pallas kernels  105 us (96%)
  local copies, waits for them, and re-layouts  3.34 us (3%)
    pallas_call x1, Pallas kernels, on_device(): pl.pallas_call(functools.partial(kernel, tiles, reps), out_shape=(out, ou...  105 us
    unnamed x2, local copies, waits for them, and re-layouts  3.34 us

profile of v2, /device:TPU:56, one launch (start us, length us, event | category | flops | bytes accessed | tf_op | source)
XLA Modules:
  0.0 108.9 jit_solution(3431791795949868218)
XLA Ops:
  0.6 104.9 %shard_map.95 = (f32[512,128]{1,0:T(8,128)}, f32[512,128]{1,0:T(8,128)}) custom-call(f32[4,4]{1,0:T(4,128)} %stack_ref.1, f32[4,4]{1,0:T(4,128)} %hairpin_ref.1, f32[31,31]{1,0:T(8,128)} %loop_ref.1, s32[324,128]{1,0:T(8,128)} %bitcast.7, s32[512,128]{1,0:T(8,128)} %allowed_hbm.1, f32[542,512]{1,0:T(8,128)} %bitcast.6, f32[8192,128]{1,0:T(8,128)} %bitcast.4, ...), custom_call_target="tpu_custom_call" | custom-call | tf_op jit(solution)/shard_map/pallas_call | solution.py:317
  105.6 1.7 %copy.12 = f32[512,128]{1,0:T(8,128)} copy(f32[512,128]{1,0:T(8,128)} %get-tuple-element.4) | data formatting | bytes 524288
  107.2 1.7 %copy.13 = f32[512,128]{1,0:T(8,128)} copy(f32[512,128]{1,0:T(8,128)} %get-tuple-element.5) | data formatting | bytes 524288

commit v3 on v2

--- a/solution.py
+++ b/solution.py
@@ -10,6 +10,7 @@
 LOOP = 30
 SPAN = 8192
 LANES = 128
+PIECES = 2
 RIM = 32
 MESH = pl.DeviceIdType.MESH
 F32 = jnp.float32
@@ -289,6 +290,29 @@
     pltpu.make_async_copy(sent, sent, sum_send).wait()
 
 
+def hand_on(paired_in, split_in, paired_out, split_out, held, in_sem, out_sem):
+    count = held.shape[1]
+    size = held.shape[2]
+
+    def ways(which, piece):
+        source, target = ((paired_in, paired_out), (split_in, split_out))[which]
+        at = pl.ds(piece * size, size)
+        here = held.at[which, piece]
+        return (
+            pltpu.make_async_copy(source.at[at], here, in_sem.at[which, piece]),
+            pltpu.make_async_copy(here, target.at[at], out_sem),
+        )
+
+    places = [(which, piece) for which in range(2) for piece in range(count)]
+    for place in places:
+        ways(*place)[0].start()
+    for place in places:
+        fetch, store = ways(*place)
+        fetch.wait()
+        store.start()
+    pltpu.make_async_copy(held, held, out_sem).wait()
+
+
 def on_device(
     tiles,
     reps,
@@ -314,7 +338,7 @@
     block = (row_count, LANES)
     pairs = (panel_count // 2, row_count, 2 * LANES)
     dma = pltpu.SemaphoreType.DMA
-    return pl.pallas_call(
+    results = pl.pallas_call(
         functools.partial(kernel, tiles, reps),
         out_shape=(out, out),
         in_specs=[smem, smem, vmem] + [any_space] * 5,
@@ -345,6 +369,18 @@
             collective_id=0, has_side_effects=True, vmem_limit_bytes=60 << 20
         ),
     )(stack_weight, hairpin_weight, loop_weight, codes, pair_allowed, inner, left, right)
+    return pl.pallas_call(
+        hand_on,
+        out_shape=(out, out),
+        in_specs=[any_space] * 2,
+        out_specs=(any_space, any_space),
+        scratch_shapes=[
+            pltpu.VMEM((2, PIECES, row_count // PIECES, cols_local), F32),
+            dma((2, PIECES)),
+            dma,
+        ],
+        compiler_params=pltpu.CompilerParams(vmem_limit_bytes=60 << 20),
+    )(*results)
 
 
 def solution(mesh):

time: 109 us -> 108 us (level)
  local copies, waits for them, and re-layouts: 3.34 us -> 0 us
  Pallas kernels: 105 us -> 107 us
    unnamed x2 -> x0, local copies, waits for them, and re-layouts: 3.34 us -> none
    pallas_call x0 -> x1, Pallas kernels: none -> 1.79 us  [on_device(): pl.pallas_call(hand_on, out_shape=(out, out), in_specs=[any_space] * 2, o...]
where the time goes in v3:
time: 108 us; the launch traced here: 107 us
  Pallas kernels  107 us (99%)
    pallas_call x1, Pallas kernels, on_device(): pl.pallas_call(functools.partial(kernel, tiles, reps), out_shape=(out, ou...  105 us

profile of v3, /device:TPU:56, one launch (start us, length us, event | category | flops | bytes accessed | tf_op | source)
XLA Modules:
  0.0 107.4 jit_solution(15443729329195610752)
XLA Ops:
  0.6 104.9 %shard_map.95 = (f32[512,128]{1,0:T(8,128)}, f32[512,128]{1,0:T(8,128)}) custom-call(f32[4,4]{1,0:T(4,128)} %stack_ref.1, f32[4,4]{1,0:T(4,128)} %hairpin_ref.1, f32[31,31]{1,0:T(8,128)} %loop_ref.1, s32[324,128]{1,0:T(8,128)} %bitcast.7, s32[512,128]{1,0:T(8,128)} %allowed_hbm.1, f32[542,512]{1,0:T(8,128)} %bitcast.6, f32[8192,128]{1,0:T(8,128)} %bitcast.4, ...), custom_call_target="tpu_custom_call" | custom-call | tf_op jit(solution)/shard_map/pallas_call | solution.py:341
  105.6 1.8 %shard_map.96 = (f32[512,128]{1,0:T(8,128)}, f32[512,128]{1,0:T(8,128)}) custom-call(f32[512,128]{1,0:T(8,128)} %get-tuple-element.4.paired_in, f32[512,128]{1,0:T(8,128)} %get-tuple-element.5.split_in), custom_call_target="tpu_custom_call" | custom-call | tf_op jit(solution)/shard_map/pallas_call | solution.py:372

commit v4 on v2

--- a/solution.py
+++ b/solution.py
@@ -10,6 +10,7 @@
 LOOP = 30
 SPAN = 8192
 LANES = 128
+PIECES = 2
 RIM = 32
 MESH = pl.DeviceIdType.MESH
 F32 = jnp.float32
@@ -37,9 +38,9 @@
 def kernel(
     tiles,
     reps,
-    stack_ref,
-    hairpin_ref,
-    loop_ref,
+    stack_hbm,
+    hairpin_hbm,
+    loop_hbm,
     codes_hbm,
     allowed_hbm,
     inner_hbm,
@@ -67,6 +68,9 @@
     rim_recv,
     sum_send,
     sum_recv,
+    stack_ref,
+    hairpin_ref,
+    loop_ref,
 ):
     tile = lax.axis_index("tile")
     rep = lax.axis_index("rep")
@@ -100,6 +104,13 @@
     fetch_right.start()
     fetch_codes.start()
     fetch_allowed.start()
+    small = ((stack_hbm, stack_ref), (hairpin_hbm, hairpin_ref), (loop_hbm, loop_ref))
+    fetch_small = [
+        pltpu.make_async_copy(source, target, local_sem.at[7 + at])
+        for at, (source, target) in enumerate(small)
+    ]
+    for fetch in fetch_small:
+        fetch.start()
     pl.semaphore_wait(barrier, panel_count - 1 + reps - 1)
 
     def columns(block):
@@ -204,6 +215,8 @@
         rows[row_count : row_count + RIM, :] = jnp.zeros((RIM, 2 * LANES), F32)
 
     sum_copy(0).start()
+    for fetch in fetch_small:
+        fetch.wait()
     weights[...] = jnp.zeros_like(weights)
     weights[0 : LOOP + 1, 0 : LOOP + 1] = loop_ref[...]
     interior[...] = jnp.zeros_like(interior)
@@ -289,6 +302,17 @@
     pltpu.make_async_copy(sent, sent, sum_send).wait()
 
 
+def hand_on(paired_in, split_in, paired_out, split_out, out_sem):
+    copies = [
+        pltpu.make_async_copy(paired_in, paired_out, out_sem.at[0]),
+        pltpu.make_async_copy(split_in, split_out, out_sem.at[1]),
+    ]
+    for copy in copies:
+        copy.start()
+    for copy in copies:
+        copy.wait()
+
+
 def on_device(
     tiles,
     reps,
@@ -309,15 +333,13 @@
     right = branch_right[0]
     out = jax.ShapeDtypeStruct((row_count, cols_local), F32)
     any_space = pl.BlockSpec(memory_space=pl.ANY)
-    smem = pl.BlockSpec(memory_space=pltpu.SMEM)
-    vmem = pl.BlockSpec(memory_space=pltpu.VMEM)
     block = (row_count, LANES)
     pairs = (panel_count // 2, row_count, 2 * LANES)
     dma = pltpu.SemaphoreType.DMA
-    return pl.pallas_call(
+    results = pl.pallas_call(
         functools.partial(kernel, tiles, reps),
         out_shape=(out, out),
-        in_specs=[smem, smem, vmem] + [any_space] * 5,
+        in_specs=[any_space] * 8,
         out_specs=(any_space, any_space),
         scratch_shapes=[
             pltpu.VMEM(codes.shape, jnp.int32),
@@ -333,18 +355,31 @@
             pltpu.VMEM(right.shape, F32),
             pltpu.VMEM((reps,) + block, F32),
             pltpu.VMEM((reps - 1,) + block, F32),
-            dma((7,)),
+            dma((10,)),
             dma,
             dma((panel_count // 2, reps)),
             dma,
             dma,
             dma,
             dma((reps - 1,)),
+            pltpu.SMEM(stack_weight.shape, F32),
+            pltpu.SMEM(hairpin_weight.shape, F32),
+            pltpu.VMEM(loop_weight.shape, F32),
         ],
         compiler_params=pltpu.CompilerParams(
-            collective_id=0, has_side_effects=True, vmem_limit_bytes=60 << 20
+            collective_id=0, has_side_effects=True, vmem_limit_bytes=53 << 20
         ),
-    )(stack_weight, hairpin_weight, loop_weight, codes, pair_allowed, inner, left, right)
+    )(*[pltpu.with_memory_space_constraint(x, pltpu.HBM) for x in (stack_weight, hairpin_weight, loop_weight, codes, pair_allowed, inner, left, right)])
+    return pl.pallas_call(
+        hand_on,
+        out_shape=(out, out),
+        in_specs=[any_space] * 2,
+        out_specs=(any_space, any_space),
+        scratch_shapes=[
+            dma((2,)),
+        ],
+        compiler_params=pltpu.CompilerParams(vmem_limit_bytes=16 << 20),
+    )(*results)
 
 
 def solution(mesh):

time: 109 us -> 105 us (0.963)
  local copies, waits for them, and re-layouts: 3.34 us -> 0 us
    unnamed x2 -> x0, local copies, waits for them, and re-layouts: 3.34 us -> none
    pallas_call x1, Pallas kernels: 105 us -> 104 us  [on_device(): pl.pallas_call(functools.partial(kernel, tiles, reps), out_shape=(out, ou...]
where the time goes in v4:
time: 105 us
  Pallas kernels  104 us (99%)
    pallas_call x1, Pallas kernels, on_device(): pl.pallas_call(functools.partial(kernel, tiles, reps), out_shape=(out, ou...  104 us

profile of v4, /device:TPU:56, one launch (start us, length us, event | category | flops | bytes accessed | tf_op | source)
XLA Modules:
  0.0 105.0 jit_solution(6206828094086340828)
XLA Ops:
  0.6 103.6 %shard_map.95 = (f32[512,128]{1,0:T(8,128)S(1)}, f32[512,128]{1,0:T(8,128)S(1)}) custom-call(f32[4,4]{1,0:T(4,128)} %stack_hbm.1, f32[4,4]{1,0:T(4,128)} %hairpin_hbm.1, f32[31,31]{1,0:T(8,128)} %loop_hbm.1, s32[324,128]{1,0:T(8,128)} %bitcast.7, s32[512,128]{1,0:T(8,128)} %allowed_hbm.1, f32[542,512]{1,0:T(8,128)} %bitcast.6, f32[8192,128]{1,0:T(8,128)} %bitcast.4, ...), custom_call_target="tpu_custom_call" | custom-call | tf_op jit(solution)/shard_map/pallas_call | solution.py:339
  104.2 0.8 shard_map.96

commit v5 on v4

--- a/solution.py
+++ b/solution.py
@@ -291,9 +291,13 @@
 
     for block in range(reps - 1):
         sum_copy(block).wait_recv()
-    sums[reps - 1] = (sums[reps - 1] + others[0]) + (others[1] + others[2])
-    store_split = pltpu.make_async_copy(sums.at[reps - 1], split_hbm, local_sem.at[6])
-    store_split.start()
+    own = sums.at[reps - 1]
+    half = row_count // 2
+    for part in range(2):
+        at = slice(part * half, (part + 1) * half)
+        own[at] = (own[at] + others[0, at]) + (others[1, at] + others[2, at])
+        pltpu.make_async_copy(own.at[at], split_hbm.at[at], local_sem.at[6]).start()
+    store_split = pltpu.make_async_copy(own, split_hbm, local_sem.at[6])
     store_paired.wait()
     store_split.wait()
     rim_copy.wait_send()

time: 105 us -> 105 us (level)
  no operation moved by 1% of the time
where the time goes in v5:
time: 105 us
  Pallas kernels  105 us (100%)
    pallas_call x1, Pallas kernels, on_device(): pl.pallas_call(functools.partial(kernel, tiles, reps), out_shape=(out, ou...  104 us

profile of v5, /device:TPU:56, one launch (start us, length us, event | category | flops | bytes accessed | tf_op | source)
XLA Modules:
  0.0 105.4 jit_solution(13083073582048066237)
XLA Ops:
  0.6 103.9 %shard_map.95 = (f32[512,128]{1,0:T(8,128)S(1)}, f32[512,128]{1,0:T(8,128)S(1)}) custom-call(f32[4,4]{1,0:T(4,128)} %stack_hbm.1, f32[4,4]{1,0:T(4,128)} %hairpin_hbm.1, f32[31,31]{1,0:T(8,128)} %loop_hbm.1, s32[324,128]{1,0:T(8,128)} %bitcast.7, s32[512,128]{1,0:T(8,128)} %allowed_hbm.1, f32[542,512]{1,0:T(8,128)} %bitcast.6, f32[8192,128]{1,0:T(8,128)} %bitcast.4, ...), custom_call_target="tpu_custom_call" | custom-call | tf_op jit(solution)/shard_map/pallas_call | solution.py:343
  104.6 0.8 shard_map.96
